TPU v7x, 256 devices: a whole 4x4x8 slice. The times are simulated.
256 devices in a mesh: tp: 2 (over z_lo), sp: 32 (over x, y, core), dp: 4 (over z_hi).
Axes of the slice: x: 4, y: 4, z: 8 (z_hi: 4, z_lo: 2; z = z_hi * 2 + z_lo), core: 2. Of those that a mesh axis runs over, the one named last changes fastest.
Arguments:
- queries: bfloat16 [16384, 4096], P(('dp', 'sp'), 'tp'), parts along dimension 0, may hold values from -256 to 256
- key_projection_rows: bfloat16 [16384, 512], P(('dp', 'sp'), 'tp'), parts along dimension 0, may hold values from -8 to 8
- values: bfloat16 [16384, 512], P(('dp', 'sp'), 'tp'), parts along dimension 0, may hold values from -6 to 6
- segment_ids: int32 [16384], P('dp'), parts along dimension 0, may hold values from 0 to 11, never falling along the last dimension, each value on 1 to 1024 neighbouring positions
- residual: bfloat16 [16384, 8192], P(('dp', 'tp'), 'sp'), parts along dimension 0, may hold values from -40 to 40
- out_weight: bfloat16 [4096, 8192], P('tp', 'sp'), may hold values from -0.09375 to 0.09375
- norm_gain: float32 [8192], P('sp'), may hold values from 0.1 to 1.9
- scale_exponent: int32 [8192], P('sp'), may hold values from 7 to 8
Outputs:
- hidden_out: bfloat16 [16384, 8192], P(('dp', 'tp'), 'sp'), parts along dimension 0
- quantized: bfloat16 [16384, 8192], P(('dp', 'tp'), 'sp'), parts along dimension 0
There are 4 independent parts, one for each index of `dp`. A program takes and returns all parts, laid end to end along the dimension named above; an argument that names none is the same for every part. Nothing has to cross between parts.
Inputs may be any that keep to these rules, and one draw needn't show every extreme that they name: `segment_ids`: never falls along the window; every document holds at most a quarter of the window's tokens, and one holds exactly that many.
All inputs are finite; a program needn't handle non-finite values.
Results may differ from a plain program's by a relative error of at most 0.0065.
Values may be sent and summed in bfloat16 or wider, within the bound.
No kernel may reach another device: no remote copies, remote signals or barrier semaphores. Data moves between devices by JAX's collectives and lax.ppermute only.
A program may use at most 64 MiB of HBM per device.

v0:
```python
import jax
import jax.numpy as jnp
from jax import lax
from jax.sharding import PartitionSpec as P

D = 8192
QUERY_HEAD_COUNT = 32
KEY_VALUE_HEADS = 4
HEAD_DIMENSION = 128
epsilon = 1e-05
limit_value = 448.0


def attend_item(query_block, key_block, value_block, query_pos, query_seg, segment_ids, key_pos):
    query_count = query_block.shape[0]
    block_rows = min(512, query_count)
    blocks = query_count // block_rows

    def one_block(packed):
        block_query, block_pos, block_seg = packed
        scores = lax.dot_general(
            block_query, key_block, (((1,), (1,)), ((), ())), preferred_element_type=jnp.float32
        ) * HEAD_DIMENSION ** (-0.5)
        visible = (key_pos[None, :] <= block_pos[:, None]) & (
            segment_ids[None, :] == block_seg[:, None]
        )
        scores = jnp.where(visible, scores, -1e30)
        largest = jnp.max(scores, axis=1, keepdims=True)
        weights = jnp.exp(scores - largest)
        row_total = jnp.sum(weights, axis=1, keepdims=True)
        probabilities = (weights / row_total).astype(jnp.bfloat16)
        return jnp.dot(probabilities, value_block, preferred_element_type=jnp.float32).astype(
            jnp.bfloat16
        )

    results = lax.map(
        one_block,
        (
            query_block.reshape(blocks, block_rows, HEAD_DIMENSION),
            query_pos.reshape(blocks, block_rows),
            query_seg.reshape(blocks, block_rows),
        ),
    )
    return results.reshape(query_count, HEAD_DIMENSION)


def body(
    queries,
    key_projection_rows,
    values,
    segment_ids,
    residual,
    out_weight,
    norm_gain,
    scale_exponent,
):
    sp_count = lax.axis_size("sp")
    token_rows = queries.shape[0]
    half_rows = token_rows // 2
    local_heads = queries.shape[1] // HEAD_DIMENSION
    item_count = 2 * local_heads
    per_device = item_count // sp_count
    window_token_rows = token_rows * sp_count
    query_count = window_token_rows // 2
    group_width = QUERY_HEAD_COUNT // KEY_VALUE_HEADS
    own_index = lax.axis_index("sp")
    query_items = jnp.transpose(
        queries.reshape(2, half_rows, local_heads, HEAD_DIMENSION), (0, 2, 1, 3)
    ).reshape(item_count, half_rows, HEAD_DIMENSION)
    query_recv = lax.all_to_all(query_items, "sp", split_axis=0, concat_axis=1, tiled=True)
    key_all, value_all = (
        lax.all_gather(key_projection_rows, "sp", axis=0, tiled=True),
        lax.all_gather(values, "sp", axis=0, tiled=True),
    )
    key_pos = jnp.arange(window_token_rows, dtype=jnp.int32)
    row_number = jnp.arange(query_count, dtype=jnp.int32)
    source_device = row_number // half_rows
    within = row_number % half_rows
    segment_grid = segment_ids.reshape(sp_count, 2, half_rows)
    number = 0
    item_index = own_index * per_device + number
    which_half = item_index // local_heads
    query_pos = source_device * token_rows + which_half * half_rows + within
    query_seg = lax.dynamic_index_in_dim(segment_grid, which_half, 1, keepdims=False).reshape(
        query_count
    )
    shared_rows = item_index % local_heads // group_width
    key_block = lax.dynamic_slice_in_dim(key_all, shared_rows * HEAD_DIMENSION, HEAD_DIMENSION, 1)
    value_block = lax.dynamic_slice_in_dim(
        value_all, shared_rows * HEAD_DIMENSION, HEAD_DIMENSION, 1
    )
    outputs = [
        attend_item(
            query_recv[number], key_block, value_block, query_pos, query_seg, segment_ids, key_pos
        )
    ]
    own_outputs = jnp.stack(outputs)
    column_count = out_weight.shape[1]
    start_sum = jnp.zeros((sp_count, 2, half_rows, column_count), jnp.float32)
    pieces = lax.all_gather(own_outputs, "sp", axis=0, tiled=True)

    def add_one(number, current):
        head_number = number % local_heads
        which_half = number // local_heads
        head_weight = lax.dynamic_slice_in_dim(
            out_weight, head_number * HEAD_DIMENSION, HEAD_DIMENSION, 0
        )
        chosen = lax.dynamic_index_in_dim(pieces, number, 0, keepdims=False)
        product_term = jnp.dot(chosen, head_weight, preferred_element_type=jnp.float32).reshape(
            sp_count, 1, half_rows, column_count
        )
        corner = (0, which_half, 0, 0)
        earlier = lax.dynamic_slice(current, corner, (sp_count, 1, half_rows, column_count))
        return lax.dynamic_update_slice(current, earlier + product_term, corner)

    combined = lax.fori_loop(0, pieces.shape[0], add_one, start_sum)
    flattened = combined.reshape(window_token_rows, column_count)
    share_rows = window_token_rows // lax.axis_size("tp")
    whole_sum = lax.psum(flattened, "tp")
    summed = lax.dynamic_slice_in_dim(whole_sum, lax.axis_index("tp") * share_rows, share_rows, 0)
    projected = summed.astype(jnp.bfloat16)
    hidden_out = (residual.astype(jnp.float32) + projected.astype(jnp.float32)).astype(jnp.bfloat16)
    widened = hidden_out.astype(jnp.float32)
    square_sum = lax.psum(jnp.sum(widened * widened, axis=1), "sp")
    mean_square = (square_sum / D)[:, None]
    normed = widened * lax.rsqrt(mean_square + epsilon) * norm_gain[None, :]
    clip_bound = (limit_value * jnp.exp2(-scale_exponent.astype(jnp.float32)))[None, :]
    quantized = jnp.clip(normed, -clip_bound, clip_bound).astype(jnp.bfloat16)
    return (hidden_out, quantized)


def solution(mesh):
    in_specs = (
        P(("dp", "sp"), "tp"),
        P(("dp", "sp"), "tp"),
        P(("dp", "sp"), "tp"),
        P("dp"),
        P(("dp", "tp"), "sp"),
        P("tp", "sp"),
        P("sp"),
        P("sp"),
    )
    out_specs = (P(("dp", "tp"), "sp"), P(("dp", "tp"), "sp"))
    return jax.shard_map(body, mesh=mesh, in_specs=in_specs, out_specs=out_specs, check_vma=False)
```

profile of v0, /device:TPU:1, one launch (start us, length us, event | category | flops | bytes accessed | tf_op | source)
XLA Modules:
  0.0 569.2 jit_solution(7606608849317972235)
XLA Ops:
  10.8 8.6 %all-to-all-start = ((bf16[32,64,128]{2,1,0:T(8,128)(2,1)}), bf16[32,64,128]{2,1,0:T(8,128)(2,1)S(1)}, u32[]{:S(2)}, u32[]{:S(2)}) async-start(bf16[32,64,128]{2,1,0:T(8,128)(2,1)} %bitcast.4), calls=%async_computation | async-start | bytes 1048576 | tf_op jit(solution)/shard_map/all_to_all | solution.py:70
  19.8 43.6 %all-gather.6.cloned.1.call-done = bf16[4096,256]{1,0:T(8,128)(2,1)} async-done(((bf16[128,256]{1,0:T(8,128)(2,1)}), bf16[4096,256]{1,0:T(8,128)(2,1)}) %all-gather.6.cloned.1.call-update) | async-done | bytes 2097168 | tf_op jit(solution)/shard_map/all_gather | solution.py:73
  64.6 49.3 %all-gather.4.cloned.1.call-done = bf16[4096,256]{1,0:T(8,128)(2,1)} async-done(((bf16[128,256]{1,0:T(8,128)(2,1)}), bf16[4096,256]{1,0:T(8,128)(2,1)}) %all-gather.4.cloned.1.call-update) | async-done | bytes 2097168 | tf_op jit(solution)/shard_map/all_gather | solution.py:72
  115.2 24.3 %while.27 = (s32[]{:T(128)}, bf16[4,512,128]{2,1,0:T(8,128)(2,1)S(1)}, s32[4,512]{1,0:T(4,128)S(1)}, s32[4096]{0:T(1024)S(1)}, s32[4,512]{1,0:T(4,128)S(1)}, /*i...) while((s32[]{:T(128)}, ...), condition=%wide.region_3.4_spmd.clone, body=%wide.region_0.3_spmd.clone.sunk | while | flops 1096875008 | bytes 27564136 | solution.py:36
  140.3 77.1 %all-gather.8.cloned.1.call-done = bf16[32,2048,128]{2,1,0:T(8,128)(2,1)} async-done(((bf16[1,2048,128]{2,1,0:T(8,128)(2,1)}), bf16[32,2048,128]{2,1,0:T(8,128)(2,1)}) %all-gather.8.cloned.1.call-update) | async-done | bytes 16777232 | tf_op jit(solution)/shard_map/all_gather | solution.py:100
  219.9 174.8 %while.26 = (s32[]{:T(128)}, f32[32,2,64,256]{3,2,1,0:T(8,128)}, bf16[32,2048,128]{2,1,0:T(8,128)(2,1)}, bf16[2048,256]{1,0:T(8,128)(2,1)}, s32[]{:T(128)}, /*in...) while((s32[]{:T(128)}, f32[32,2,64,256]{3,2,1,0:T(8,128)}, ...), condition=%wide.region_5.6_spmd, body=%wide.region_4.5_spmd.sunk | while | flops 134742032 | bytes 10027344 | solution.py:116
  309.6 2.6 bitcast_dynamic-update-slice_fusion.2
  315.1 2.6 bitcast_dynamic-update-slice_fusion.2
  320.6 2.6 bitcast_dynamic-update-slice_fusion.2
  326.0 2.6 bitcast_dynamic-update-slice_fusion.2
  331.5 2.6 bitcast_dynamic-update-slice_fusion.2
  337.0 2.6 bitcast_dynamic-update-slice_fusion.2
  342.5 2.6 bitcast_dynamic-update-slice_fusion.2
  348.0 2.6 bitcast_dynamic-update-slice_fusion.2
  353.5 2.6 bitcast_dynamic-update-slice_fusion.2
  359.0 2.6 bitcast_dynamic-update-slice_fusion.2
  364.5 2.6 bitcast_dynamic-update-slice_fusion.2
  370.0 2.6 bitcast_dynamic-update-slice_fusion.2
  375.5 2.6 bitcast_dynamic-update-slice_fusion.2
  381.0 2.6 bitcast_dynamic-update-slice_fusion.2
  386.5 2.6 bitcast_dynamic-update-slice_fusion.2
  392.0 2.6 bitcast_dynamic-update-slice_fusion.2
  394.7 100.2 %all-reduce.1 = bf16[4096,256]{1,0:T(8,128)(2,1)S(1)} all-reduce(f32[4096,256]{1,0:T(8,128)} %bitcast.61), channel_id=1, replica_groups=mesh['tp'=2,'sp'=32,'dp'=4] {'tp'}, use_global_device_ids=true, to_apply=%region_6.7 | all-reduce | flops 1048576 | bytes 6291456 | tf_op jit(solution)/shard_map/psum | solution.py:119
  496.6 64.7 %psum.15 = f32[2048]{0:T(1024)S(1)} all-reduce(f32[2048]{0:T(1024)S(1)} %get-tuple-element.206), channel_id=1, replica_groups=mesh['tp'=2,'sp'=32,'dp'=4] {'sp'}, use_global_device_ids=true, to_apply=%region_8.9 | all-reduce | flops 2048 | bytes 16384 | tf_op jit(solution)/shard_map/psum | solution.py:124
  (128 shorter events, 168.9 us)
Async XLA Ops:
  7.2 12.3 %copy-start.2 = (s32[4096]{0:T(1024)S(1)}, s32[4096]{0:T(1024)}, u32[]{:S(2)}) copy-start(s32[4096]{0:T(1024)} %param.15) | copy-start | bytes 49156
  7.2 56.2 %all-gather.6.cloned.1.call-start = ((), (), s32[]{:S(2)}) async-start(), calls=%async_computation.2 | async-start | bytes 2162688 | tf_op jit(solution)/shard_map/all_gather | solution.py:73
  7.9 106.0 %all-gather.4.cloned.1.call-start = ((), (), s32[]{:S(2)}) async-start(), calls=%async_computation.1 | async-start | bytes 2162688 | tf_op jit(solution)/shard_map/all_gather | solution.py:72
  10.8 104.4 %all-to-all-start = ((bf16[32,64,128]{2,1,0:T(8,128)(2,1)}), bf16[32,64,128]{2,1,0:T(8,128)(2,1)S(1)}, u32[]{:S(2)}, u32[]{:S(2)}) async-start(bf16[32,64,128]{2,1,0:T(8,128)(2,1)} %bitcast.4), calls=%async_computation | async-start | bytes 1048576 | tf_op jit(solution)/shard_map/all_to_all | solution.py:70
  19.4 198.0 %all-gather.8.cloned.1.call-start = ((), (), s32[]{:S(2)}) async-start(), calls=%async_computation.3 | async-start | bytes 17301504 | tf_op jit(solution)/shard_map/all_gather | solution.py:100
  115.2 25.1 %copy-start.4 = (s32[256]{0:T(256)S(1)}, s32[256]{0:T(256)}, u32[]{:S(2)}) copy-start(s32[256]{0:T(256)} %param.19) | copy-start | bytes 3076
  139.5 0.8 copy-start.1
  394.7 166.6 %copy-start.3 = (f32[256]{0:T(256)S(1)}, f32[256]{0:T(256)}, u32[]{:S(2)}) copy-start(f32[256]{0:T(256)} %param.18) | copy-start | bytes 3076
  496.5 66.2 %copy-start = (bf16[2048,256]{1,0:T(8,128)(2,1)}, bf16[2048,256]{1,0:T(8,128)(2,1)S(1)}, u32[]{:S(2)}) copy-start(bf16[2048,256]{1,0:T(8,128)(2,1)S(1)} %get-tuple-element.207) | copy-start | bytes 3145732
Sparse Core Ops, SparseCore 0:
  10.5 52.7 all-gather.5
  65.9 47.9 all-gather.3
  140.4 76.9 all-gather.7
where the time goes:
time: 574 us; the launch traced here: 569 us
  waiting for transfers between devices  171 us (30%)
  blocking collectives  165 us (29%)
  matrix products  103 us (18%)
  local copies, waits for them, and re-layouts  98.9 us (17%)
  between operations  14 us (2%)
  starting transfers between devices  8.69 us (2%)
  other arithmetic  8.28 us (1%)
    psum x1, blocking collectives, body(): whole_sum = lax.psum(flattened, 'tp')  100 us
    dot_general x32, matrix products, add_one(): jnp.dot(chosen, head_weight, preferred_element_type=jnp.float32)  83.6 us
    all_gather x1, waiting for transfers between devices, body(): pieces = lax.all_gather(own_outputs, 'sp', axis=0, tiled=True)  77.1 us
    psum x1, blocking collectives, body(): square_sum = lax.psum(jnp.sum(widened * widened, axis=1), 'sp')  64.7 us
    dynamic_slice x32, local copies, waits for them, and re-layouts, add_one(): lax.dynamic_slice(current, corner, (sp_count, 1, half_rows, column_count))  56.2 us
    all_gather x1, waiting for transfers between devices, body(): lax.all_gather(key_projection_rows, 'sp', axis=0, tiled=True)  49.3 us
    all_gather x1, waiting for transfers between devices, body(): lax.all_gather(values, 'sp', axis=0, tiled=True)  43.6 us
    dynamic_slice x32, local copies, waits for them, and re-layouts, add_one(): chosen = lax.dynamic_index_in_dim(pieces, number, 0, keepdims=False)  34.6 us
  transfers between devices with their start and end apart: 4, of which 3 were waited for; matrix products, arithmetic and copies ran while one was open for 1% of the time, Pallas kernels for 0%

commit v1 on v0

--- a/solution.py
+++ b/solution.py
@@ -116,7 +116,7 @@
     combined = lax.fori_loop(0, pieces.shape[0], add_one, start_sum)
     flattened = combined.reshape(window_token_rows, column_count)
     share_rows = window_token_rows // lax.axis_size("tp")
-    whole_sum = lax.psum(flattened, "tp")
+    whole_sum = jnp.sum(lax.all_gather(flattened, "tp"), axis=0)
     summed = lax.dynamic_slice_in_dim(whole_sum, lax.axis_index("tp") * share_rows, share_rows, 0)
     projected = summed.astype(jnp.bfloat16)
     hidden_out = (residual.astype(jnp.float32) + projected.astype(jnp.float32)).astype(jnp.bfloat16)

time: 574 us -> 589 us (1.026)
  waiting for transfers between devices: 171 us -> 279 us
  blocking collectives: 165 us -> 63.8 us
    all_gather x0 -> x1, waiting for transfers between devices: none -> 108 us  [body(): whole_sum = jnp.sum(lax.all_gather(flattened, 'tp'), axis=0)]
    psum x1 -> x0, blocking collectives: 100 us -> none  [body(): whole_sum = lax.psum(flattened, 'tp')]
  transfers between devices with their start and end apart: 4 -> 5, of which waited for: 3 -> 4; matrix products, arithmetic and copies ran while one was open for 1% -> 1% of each run, Pallas kernels for 0% -> 0%
where the time goes in v1:
time: 589 us; the launch traced here: 582 us
  waiting for transfers between devices  279 us (47%)
  matrix products  104 us (18%)
  local copies, waits for them, and re-layouts  99.6 us (17%)
  blocking collectives  63.8 us (11%)
  between operations  14 us (2%)
  other arithmetic  13 us (2%)
  starting transfers between devices  8.73 us (1%)
    all_gather x1, waiting for transfers between devices, body(): whole_sum = jnp.sum(lax.all_gather(flattened, 'tp'), axis=0)  108 us
    dot_general x32, matrix products, add_one(): jnp.dot(chosen, head_weight, preferred_element_type=jnp.float32)  84.6 us
    all_gather x1, waiting for transfers between devices, body(): pieces = lax.all_gather(own_outputs, 'sp', axis=0, tiled=True)  77.1 us
    psum x1, blocking collectives, body(): square_sum = lax.psum(jnp.sum(widened * widened, axis=1), 'sp')  63.8 us
    dynamic_slice x32, local copies, waits for them, and re-layouts, add_one(): lax.dynamic_slice(current, corner, (sp_count, 1, half_rows, column_count))  56.2 us
    all_gather x1, waiting for transfers between devices, body(): lax.all_gather(key_projection_rows, 'sp', axis=0, tiled=True)  49.3 us
    all_gather x1, waiting for transfers between devices, body(): lax.all_gather(values, 'sp', axis=0, tiled=True)  43.6 us
    dynamic_slice x32, local copies, waits for them, and re-layouts, add_one(): chosen = lax.dynamic_index_in_dim(pieces, number, 0, keepdims=False)  34.6 us
  transfers between devices with their start and end apart: 5, of which 4 were waited for; matrix products, arithmetic and copies ran while one was open for 1% of the time, Pallas kernels for 0%

profile of v1, /device:TPU:1, one launch (start us, length us, event | category | flops | bytes accessed | tf_op | source)
XLA Modules:
  0.0 582.2 jit_solution(13931428023203419197)
XLA Ops:
  10.8 8.6 %all-to-all-start = ((bf16[32,64,128]{2,1,0:T(8,128)(2,1)}), bf16[32,64,128]{2,1,0:T(8,128)(2,1)S(1)}, u32[]{:S(2)}, u32[]{:S(2)}) async-start(bf16[32,64,128]{2,1,0:T(8,128)(2,1)} %bitcast.4), calls=%async_computation | async-start | bytes 1048576 | tf_op jit(solution)/shard_map/all_to_all | solution.py:70
  19.8 43.6 %all-gather.7.cloned.1.call-done = bf16[4096,256]{1,0:T(8,128)(2,1)} async-done(((bf16[128,256]{1,0:T(8,128)(2,1)}), bf16[4096,256]{1,0:T(8,128)(2,1)}) %all-gather.7.cloned.1.call-update) | async-done | bytes 2097168 | tf_op jit(solution)/shard_map/all_gather | solution.py:73
  64.6 49.3 %all-gather.5.cloned.1.call-done = bf16[4096,256]{1,0:T(8,128)(2,1)} async-done(((bf16[128,256]{1,0:T(8,128)(2,1)}), bf16[4096,256]{1,0:T(8,128)(2,1)}) %all-gather.5.cloned.1.call-update) | async-done | bytes 2097168 | tf_op jit(solution)/shard_map/all_gather | solution.py:72
  115.2 24.3 %while.27 = (s32[]{:T(128)}, bf16[4,512,128]{2,1,0:T(8,128)(2,1)S(1)}, s32[4,512]{1,0:T(4,128)S(1)}, s32[4096]{0:T(1024)S(1)}, s32[4,512]{1,0:T(4,128)S(1)}, /*i...) while((s32[]{:T(128)}, ...), condition=%wide.region_3.4_spmd.clone, body=%wide.region_0.3_spmd.clone.sunk | while | flops 1096875008 | bytes 27564136 | solution.py:36
  140.3 77.1 %all-gather.9.cloned.1.call-done = bf16[32,2048,128]{2,1,0:T(8,128)(2,1)} async-done(((bf16[1,2048,128]{2,1,0:T(8,128)(2,1)}), bf16[32,2048,128]{2,1,0:T(8,128)(2,1)}) %all-gather.9.cloned.1.call-update) | async-done | bytes 16777232 | tf_op jit(solution)/shard_map/all_gather | solution.py:100
  219.8 175.8 %while.26 = (s32[]{:T(128)}, f32[32,2,64,256]{3,2,1,0:T(8,128)}, bf16[32,2048,128]{2,1,0:T(8,128)(2,1)}, bf16[2048,256]{1,0:T(8,128)(2,1)}, s32[]{:T(128)}, /*in...) while((s32[]{:T(128)}, f32[32,2,64,256]{3,2,1,0:T(8,128)}, ...), condition=%wide.region_5.6_spmd, body=%wide.region_4.5_spmd.sunk | while | flops 134742032 | bytes 10027344 | solution.py:116
  233.7 2.6 bitcast_dynamic-update-slice_fusion.2
  239.2 2.6 bitcast_dynamic-update-slice_fusion.2
  244.7 2.6 bitcast_dynamic-update-slice_fusion.2
  250.2 2.6 bitcast_dynamic-update-slice_fusion.2
  255.7 2.6 bitcast_dynamic-update-slice_fusion.2
  261.2 2.6 bitcast_dynamic-update-slice_fusion.2
  266.7 2.6 bitcast_dynamic-update-slice_fusion.2
  272.2 2.6 bitcast_dynamic-update-slice_fusion.2
  277.7 2.6 bitcast_dynamic-update-slice_fusion.2
  283.2 2.6 bitcast_dynamic-update-slice_fusion.2
  288.7 2.6 bitcast_dynamic-update-slice_fusion.2
  294.2 2.6 bitcast_dynamic-update-slice_fusion.2
  299.7 2.6 bitcast_dynamic-update-slice_fusion.2
  305.2 2.6 bitcast_dynamic-update-slice_fusion.2
  310.7 2.6 bitcast_dynamic-update-slice_fusion.2
  396.4 107.6 %all-gather.11.cloned.1.call-done = f32[2,4096,256]{2,1,0:T(8,128)} async-done(((f32[1,4096,256]{2,1,0:T(8,128)}), f32[2,4096,256]{2,1,0:T(8,128)}) %all-gather.11.cloned.1.call-update) | async-done | bytes 8388624 | tf_op jit(solution)/shard_map/all_gather | solution.py:119
  504.0 4.7 reduce_sum.27
  510.4 63.8 %psum.7 = f32[2048]{0:T(1024)S(1)} all-reduce(f32[2048]{0:T(1024)S(1)} %get-tuple-element.206), channel_id=1, replica_groups=mesh['tp'=2,'sp'=32,'dp'=4] {'sp'}, use_global_device_ids=true, to_apply=%region_8.9 | all-reduce | flops 2048 | bytes 16384 | tf_op jit(solution)/shard_map/psum | solution.py:124
  (131 shorter events, 173.2 us)
Async XLA Ops:
  7.2 12.3 %copy-start.2 = (s32[4096]{0:T(1024)S(1)}, s32[4096]{0:T(1024)}, u32[]{:S(2)}) copy-start(s32[4096]{0:T(1024)} %param.15) | copy-start | bytes 49156
  7.2 56.2 %all-gather.7.cloned.1.call-start = ((), (), s32[]{:S(2)}) async-start(), calls=%async_computation.2 | async-start | bytes 2162688 | tf_op jit(solution)/shard_map/all_gather | solution.py:73
  7.9 106.0 %all-gather.5.cloned.1.call-start = ((), (), s32[]{:S(2)}) async-start(), calls=%async_computation.1 | async-start | bytes 2162688 | tf_op jit(solution)/shard_map/all_gather | solution.py:72
  10.8 104.4 %all-to-all-start = ((bf16[32,64,128]{2,1,0:T(8,128)(2,1)}), bf16[32,64,128]{2,1,0:T(8,128)(2,1)S(1)}, u32[]{:S(2)}, u32[]{:S(2)}) async-start(bf16[32,64,128]{2,1,0:T(8,128)(2,1)} %bitcast.4), calls=%async_computation | async-start | bytes 1048576 | tf_op jit(solution)/shard_map/all_to_all | solution.py:70
  19.4 198.0 %all-gather.9.cloned.1.call-start = ((), (), s32[]{:S(2)}) async-start(), calls=%async_computation.3 | async-start | bytes 17301504 | tf_op jit(solution)/shard_map/all_gather | solution.py:100
  139.5 0.8 copy-start.1
  140.3 363.7 %all-gather.11.cloned.1.call-start = ((), (), s32[]{:S(2)}) async-start(), calls=%async_computation.4 | async-start | bytes 12582912 | tf_op jit(solution)/shard_map/all_gather | solution.py:119
  395.7 0.7 copy-start.4
  396.4 177.9 %copy-start.3 = (f32[256]{0:T(256)S(1)}, f32[256]{0:T(256)}, u32[]{:S(2)}) copy-start(f32[256]{0:T(256)} %param.18) | copy-start | bytes 3076
  510.3 65.3 %copy-start = (bf16[2048,256]{1,0:T(8,128)(2,1)}, bf16[2048,256]{1,0:T(8,128)(2,1)S(1)}, u32[]{:S(2)}) copy-start(bf16[2048,256]{1,0:T(8,128)(2,1)S(1)} %get-tuple-element.207) | copy-start | bytes 3145732
Sparse Core Ops, SparseCore 0:
  10.5 52.7 all-gather.6
  65.9 47.9 all-gather.4
  140.4 76.9 all-gather.8
  395.8 108.1 all-gather.10
